TPU v7x, 32 devices: a whole 2x2x4 slice. The times are simulated.
32 devices in a mesh: group: 2 (over x), surf: 16 (over z, y, core).
Axes of the slice: x: 2, y: 2, z: 4, core: 2. Of those that a mesh axis runs over, the one named last changes fastest.
Arguments:
- traces: bfloat16 [4096, 128, 1024], P('surf', 'group'), parts along dimension 1, may hold values from -6 to 6
- operator: bfloat16 [4096, 8, 2, 4096], P('surf'), may hold values from -1 to 1, as said below
- freq_bins: int32 [8], replicated, may hold values from 1 to 511, as said below
- win_lengths: int32 [16], replicated, may hold values from 1 to 96, 1024 in all
- coefficients: float32 [16, 31], replicated, may hold values from -2.5 to 2.5
- neighbour: int32 [4096], P('surf'), may hold values from -2 to 2, as said below
Outputs:
- demultiple: bfloat16 [4096, 128, 1024], P('surf', 'group'), parts along dimension 1
There are 2 independent parts, one for each index of `group`. A program takes and returns all parts, laid end to end along the dimension named above; an argument that names none is the same for every part. Nothing has to cross between parts.
Inputs may be any that keep to these rules, and one draw needn't show every extreme that they name: operator[i, f, c, j] equals operator[j, f, c, i] (reciprocity). `freq_bins`: the 8 bins are distinct. `neighbour`: points of even index take an offset of -2 or -1, points of odd index 1 or 2.
All inputs are finite; a program needn't handle non-finite values.
Results may differ from a plain program's by a relative error of at most 0.004.
Values may be sent and summed in bfloat16 or wider, within the bound.
A program may use at most 192 MiB of HBM per device.

v0:
```python
import math

import jax
import jax.numpy as jnp
from jax import lax
from jax.sharding import PartitionSpec as P

TAPS = 31
HALO = 2


def padded_2(x, sides, width):
    for axis, dim in sides:
        size, length = (lax.axis_size(axis), x.shape[dim])
        up = [(i, (i + 1) % size) for i in range(size - 1)]
        down = [(j, i) for i, j in up]
        last = lax.slice_in_dim(x, length - width, length, axis=dim)
        initial = lax.slice_in_dim(x, 0, width, axis=dim)
        before = lax.ppermute(last, axis, up)
        after = lax.ppermute(initial, axis, down)
        x = jnp.concatenate([before, x, after], axis=dim)
    return x


def angle_grid(freq_bins, samples):
    sample_index = jnp.arange(samples, dtype=jnp.int32)
    phases = sample_index[:, None] * freq_bins[None, :] % samples
    return 2.0 * math.pi / samples * phases.astype(jnp.float32)


def combine_complex_parts(products):
    real_part = products[:, :, 0, 0] - products[:, :, 1, 1]
    imag_part = products[:, :, 0, 1] + products[:, :, 1, 0]
    return jnp.stack([real_part, imag_part], axis=2)


def matching(multiple_estimate, coefficients, win_lengths):
    samples = multiple_estimate.shape[2]
    half_taps = (TAPS - 1) // 2
    window_ends = jnp.cumsum(win_lengths)
    sample_index = jnp.arange(samples, dtype=jnp.int32)
    window = jnp.sum((window_ends[None, :] <= sample_index[:, None]).astype(jnp.int32), axis=1)
    membership = (
        window[:, None] == jnp.arange(coefficients.shape[0], dtype=jnp.int32)[None, :]
    ).astype(jnp.float32)
    per_sample = jnp.dot(membership, coefficients, precision=lax.Precision.HIGHEST)
    padded = jnp.pad(multiple_estimate, ((0, 0), (0, 0), (half_taps, half_taps)))
    summed = jnp.zeros_like(multiple_estimate)
    for lag_index in range(TAPS):
        summed = summed + per_sample[:, lag_index] * padded[:, :, lag_index : lag_index + samples]
    return summed


def to_traces(spectral_domain, basis):
    point_count, freq_count, parts_count, shot_count = spectral_domain.shape
    rows = spectral_domain.transpose(0, 3, 1, 2).reshape(
        point_count * shot_count, freq_count * parts_count
    )
    timed = jnp.dot(rows, basis, precision=lax.Precision.HIGHEST)
    return timed.reshape(point_count, shot_count, basis.shape[1])


def neighbour_mix(central, padded, neighbour):
    row_count = central.shape[0]
    summed = central
    for offset in range(-HALO, HALO + 1):
        selector = (
            (neighbour == offset)
            .astype(jnp.float32)
            .reshape((row_count,) + (1,) * (central.ndim - 1))
        )
        summed = summed + 0.5 * selector * padded[HALO + offset : HALO + offset + row_count]
    return summed


def on_device(traces, operator, freq_bins, win_lengths, coefficients, neighbour):
    local_points, shot_count, samples = traces.shape
    freq_count = freq_bins.shape[0]
    angles = angle_grid(freq_bins, samples)
    forward = (
        jnp.stack([jnp.cos(angles), -jnp.sin(angles)], axis=2)
        .reshape(samples, 2 * freq_count)
        .astype(jnp.bfloat16)
    )
    spectra = jnp.dot(
        traces.reshape(local_points * shot_count, samples),
        forward,
        preferred_element_type=jnp.float32,
    ).astype(jnp.bfloat16)
    spectra = spectra.reshape(local_points, shot_count, freq_count, 2).transpose(0, 2, 3, 1)
    products = jnp.einsum("cfar,cfbs->rfabs", operator, spectra, preferred_element_type=jnp.float32)
    predicted_multiples = lax.psum_scatter(
        combine_complex_parts(products).reshape(
            lax.axis_size("surf") * local_points, freq_count * 2 * shot_count
        ),
        "surf",
        scatter_dimension=0,
        tiled=True,
    )
    predicted_multiples = predicted_multiples.reshape(local_points, freq_count, 2, shot_count)
    norm_divisor = (2.0 * freq_count * samples) ** (-0.5)
    inverse_transform = norm_divisor * jnp.stack([jnp.cos(angles.T), -jnp.sin(angles.T)], axis=1)
    basis = matching(
        inverse_transform.reshape(2 * freq_count, 1, samples), coefficients, win_lengths
    ).reshape(2 * freq_count, samples)
    padded = padded_2(predicted_multiples.astype(jnp.bfloat16), (("surf", 0),), HALO).astype(
        predicted_multiples.dtype
    )
    mixed = neighbour_mix(predicted_multiples, padded, neighbour)
    adapted = to_traces(mixed, basis)
    return (traces.astype(jnp.float32) - adapted).astype(jnp.bfloat16)


def solution(mesh):
    return jax.shard_map(
        on_device,
        mesh=mesh,
        in_specs=(P("surf", "group", None), P("surf", None, None, None), P(), P(), P(), P("surf")),
        out_specs=P("surf", "group", None),
        check_vma=False,
    )
```

profile of v0, /device:TPU:0, one launch (start us, length us, event | category | flops | bytes accessed | tf_op | source)
XLA Modules:
  0.0 426.8 jit_solution(694189632699482941)
XLA Ops:
  6.5 0.0 copy-start
  6.5 0.0 reduce-scatter.2.cloned.1.call-start
  6.5 0.9 cosine_convert_fusion
  7.5 14.1 %fusion.2 = bf16[16384,16]{0,1:T(8,128)(2,1)S(1)} fusion(bf16[1024,16]{0,1:T(8,128)(2,1)S(1)} %convert_element_type.69, bf16[16384,1024]{1,0:T(8,128)(2,1)} %bitcast.77), kind=kOutput, calls=%fused_computation.4 | convolution fusion | flops 537133056 | bytes 34111488 | tf_op jit(solution)/shard_map/dot_general | solution.py:85
  21.6 1.1 reshape.430
  22.7 32.5 %fusion.3 = f32[4096,8,2,2,64]{0,4,2,3,1:T(8,128)} fusion(bf16[256,8,2,4096,1]{3,2,1,0,4:T(2,128)(2,1)} %bitcast.79, bf16[256,64,8,2]{1,0,3,2:T(8,128)(2,1)S(1)} %reshape.430), kind=kOutput, calls=%fused_computation.6 | convolution fusion | flops 4294967296 | bytes 67633152 | tf_op jit(solution)/shard_map/cfar,cfbs->rfabs/dot_general | solution.py:91
  55.2 11.1 %fusion.6 = f32[4096,8,1,64]{0,3,1,2:T(8,128)} fusion(f32[4096,8,2,2,64]{0,4,2,3,1:T(8,128)} %fusion.3), kind=kLoop, calls=%fused_computation.8 | loop fusion | flops 2097152 | bytes 25165824 | tf_op jit(solution)/shard_map/add | solution.py:33
  66.3 11.1 %fusion.8 = f32[4096,8,1,64]{0,3,1,2:T(8,128)} fusion(f32[4096,8,2,2,64]{0,4,2,3,1:T(8,128)} %fusion.3), kind=kLoop, calls=%fused_computation.11 | loop fusion | flops 2097152 | bytes 25165824 | tf_op jit(solution)/shard_map/sub | solution.py:32
  77.5 6.6 %pad_maximum_fusion = f32[4096,8,2,64]{0,3,1,2:T(8,128)S(1)} fusion(f32[4096,8,1,64]{0,3,1,2:T(8,128)} %fusion.6, f32[4096,8,1,64]{0,3,1,2:T(8,128)} %fusion.8), kind=kLoop, calls=%fused_computation.5 | loop fusion | flops 4194304 | bytes 33554432 | tf_op jit(solution)/shard_map/stack | solution.py:34
  84.1 6.2 %copy.48 = f32[4096,8,2,64]{0,3,2,1:T(8,128)} copy(f32[4096,8,2,64]{0,3,1,2:T(8,128)S(1)} %pad_maximum_fusion) | data formatting | bytes 33554432 | tf_op jit(solution)/shard_map/stack | solution.py:34
  90.3 0.0 copy-start.3
  90.3 0.0 copy-start.1
  90.3 0.0 copy-start.2
  90.3 0.0 reduce-scatter.2.cloned.1.call-update
  90.3 0.6 copy-done.3
  90.9 0.1 copy.49
  91.1 0.1 reduce
  91.2 0.0 copy-done.1
  91.2 0.2 fusion.130
  91.4 0.1 copy.50
  91.5 0.1 convert_reduce_fusion
  91.6 0.0 copy-done
  91.6 0.5 fusion.16
  92.2 0.1 fusion.133
  92.3 178.0 %reduce-scatter.2.cloned.1.call-done = f32[256,1024]{0,1:T(8,128)} async-done(((f32[4096,1024]{0,1:T(8,128)}), f32[256,1024]{0,1:T(8,128)}) %reduce-scatter.2.cloned.1.call-update) | async-done | bytes 1048592 | tf_op jit(solution)/shard_map/reduce_scatter | solution.py:92
  270.3 1.3 convert_element_type.72
  271.6 0.1 fusion.132
  271.7 1.5 collective-permute-start
  273.2 1.3 collective-permute-start.1
  274.5 0.0 copy-done.2
  274.5 0.0 collective-permute-done
  274.5 3.6 collective-permute-done.1
  278.2 0.5 maximum_convert_fusion
  278.7 2.4 fusion.9
  281.1 108.1 %subtract_convert_fusion = bf16[256,64,1024]{2,0,1:T(8,128)(2,1)} fusion(bf16[256,64,1024]{2,1,0:T(8,128)(2,1)} %param.6, f32[256,64,16]{0,1,2:T(8,128)S(1)} %bitcast.80, f32[16,1,1024]{2,0,1:T(8,128)S(1)} %broadcast_multiply_fusion, f32[16,1,1024]{2,0,1:T(8,128)S(1)} %stack.21, f32[1024]{0:T(1024)S(1)} %bitcast.96, f32[1024]{0:T(1024)S(1)} %bitcast.97, ...), kind=kOutput, calls=%fused_computation | convolution fusion | flops 3272556544 | bytes 68415488 | tf_op jit(solution)/shard_map/dot_general | solution.py:59
  389.2 30.8 %copy.52 = bf16[256,64,1024]{2,1,0:T(8,128)(2,1)} copy(bf16[256,64,1024]{2,0,1:T(8,128)(2,1)} %subtract_convert_fusion) | data formatting | bytes 67108864 | tf_op jit(solution)/shard_map/convert_element_type | solution.py:111
  (9 shorter events, 0.2 us)
Async XLA Ops:
  6.5 85.1 %copy-start = (f32[16,31]{1,0:T(8,128)S(1)}, f32[16,31]{1,0:T(8,128)}, u32[]{:S(2)}) copy-start(f32[16,31]{1,0:T(8,128)} %param.10) | copy-start | bytes 5956
  6.5 263.8 %reduce-scatter.2.cloned.1.call-start = ((), (), s32[]{:S(2)}) async-start(), calls=%async_computation.1 | async-start | bytes 17825792 | tf_op jit(solution)/shard_map/reduce_scatter | solution.py:92
  90.3 0.7 copy-start.3
  90.3 0.9 copy-start.1
  90.3 184.2 %copy-start.2 = (s32[256]{0:T(256)S(1)}, s32[256]{0:T(256)}, u32[]{:S(2)}) copy-start(s32[256]{0:T(256)} %param.11) | copy-start | bytes 3076
  271.7 2.8 collective-permute-start
  273.2 5.0 %collective-permute-start.1 = (bf16[2,8,2,64]{0,3,2,1:T(8,128)(2,1)S(1)}, bf16[2,8,2,64]{0,3,2,1:T(8,128)(2,1)S(1)}, u32[]{:S(2)}, u32[]{:S(2)}) collective-permute-start(bf16[2,8,2,64]{0,3,2,1:T(8,128)(2,1)S(1)} %get-tuple-element.6), channel_id=1, source_target_pairs={{1,0},{2,1},{3,2},{4,3},{5,4},{6,5},{7,6},{8,7},{9,8},{10,9},{11,1... | collective-permute-start | bytes 12296 | tf_op jit(solution)/shard_map/ppermute | solution.py:20
Sparse Core Ops, SparseCore 0:
  90.4 179.8 reduce-scatter.1
where the time goes:
time: 431 us; the launch traced here: 427 us
  waiting for transfers between devices  182 us (42%)
  matrix products  155 us (36%)
  local copies, waits for them, and re-layouts  39.2 us (9%)
  other arithmetic  34.4 us (8%)
  between operations  13.6 us (3%)
    reduce_scatter x1, waiting for transfers between devices, on_device(): lax.psum_scatter(combine_complex_parts(products).reshape(lax.axis_size('s...  178 us
    dot_general x1, matrix products, to_traces(): timed = jnp.dot(rows, basis, precision=lax.Precision.HIGHEST)  108 us
    dot_general x1, matrix products, on_device(): jnp.einsum('cfar,cfbs->rfabs', operator, spectra, preferred_element_type=...  32.5 us
    convert_element_type x1, local copies, waits for them, and re-layouts, on_device(): return (traces.astype(jnp.float32) - adapted).astype(jnp.bfloat16)  30.8 us
    dot_general x1, matrix products, on_device(): jnp.dot(traces.reshape(local_points * shot_count, samples), forward, pref...  14.1 us
    sub x1, other arithmetic, combine_complex_parts(): real_part = products[:, :, 0, 0] - products[:, :, 1, 1]  11.1 us
    add x1, other arithmetic, combine_complex_parts(): imag_part = products[:, :, 0, 1] + products[:, :, 1, 0]  11.1 us
  transfers between devices with their start and end apart: 3, of which 2 were waited for; matrix products, arithmetic and copies ran while one was open for 0% of the time, Pallas kernels for 0%

commit v1 on v0

v1 whole, which is shorter than its diff:
```python
import functools
import math

import jax
import jax.numpy as jnp
from jax import lax
from jax.experimental import pallas as pl
from jax.experimental.pallas import tpu as pltpu
from jax.sharding import PartitionSpec as P

TAPS = 31
HALO = 2
VMEM_LIMIT = 60 * 1024 * 1024
NT_DIMS = (((1,), (1,)), ((), ()))
TN_DIMS = (((0,), (0,)), ((), ()))


def angle_grid(freq_bins, samples):
    sample_index = jnp.arange(samples, dtype=jnp.int32)
    phases = sample_index[:, None] * freq_bins[None, :] % samples
    return 2.0 * math.pi / samples * phases.astype(jnp.float32)


def matching(multiple_estimate, coefficients, win_lengths):
    samples = multiple_estimate.shape[1]
    half_taps = (TAPS - 1) // 2
    window_ends = jnp.cumsum(win_lengths)
    sample_index = jnp.arange(samples, dtype=jnp.int32)
    window = jnp.sum((window_ends[None, :] <= sample_index[:, None]).astype(jnp.int32), axis=1)
    membership = (
        window[None, :] == jnp.arange(coefficients.shape[0], dtype=jnp.int32)[:, None]
    ).astype(jnp.float32)
    per_sample = jnp.dot(coefficients.T, membership, precision=lax.Precision.HIGHEST)
    padded = jnp.pad(multiple_estimate, ((0, 0), (half_taps, half_taps)))
    summed = jnp.zeros_like(multiple_estimate)
    for lag_index in range(TAPS):
        summed = summed + per_sample[lag_index][None] * padded[:, lag_index : lag_index + samples]
    return summed


def swap_halves(x, half):
    return pltpu.roll(x, half, axis=1)


def forward_kernel(freq_count, shots, traces_ref, table_ref, out_ref, lines):
    points = out_ref.shape[1]
    lanes = 2 * shots
    spectra = lax.dot_general(
        table_ref[...], traces_ref[...], NT_DIMS, preferred_element_type=jnp.float32
    )
    low = lax.broadcasted_iota(jnp.int32, (freq_count, lanes), 1) < shots
    for pair in range(points // 2):
        cols = slice(pair * lanes, (pair + 1) * lanes)
        real, imag = spectra[:freq_count, cols], spectra[freq_count:, cols]
        first = jnp.where(low, real, swap_halves(imag, shots))
        second = jnp.where(low, swap_halves(real, shots), imag)
        at = 2 * pair * freq_count
        lines[at : at + freq_count, :] = first
        lines[at + freq_count : at + 2 * freq_count, :] = second
    for f in range(freq_count):
        out_ref[f] = lines[pl.ds(f, points, stride=freq_count), :].astype(out_ref.dtype)


def forward(traces2, table, freq_count, shots, points):
    rows, samples = traces2.shape
    local = rows // shots
    return pl.pallas_call(
        functools.partial(forward_kernel, freq_count, shots),
        out_shape=jax.ShapeDtypeStruct((freq_count, local, 2 * shots), jnp.bfloat16),
        grid=(local // points,),
        in_specs=[
            pl.BlockSpec((points * shots, samples), lambda i: (i, 0)),
            pl.BlockSpec((2 * freq_count, samples), lambda i: (0, 0)),
        ],
        out_specs=pl.BlockSpec((freq_count, points, 2 * shots), lambda i: (0, i, 0)),
        scratch_shapes=[pltpu.VMEM((points * freq_count, 2 * shots), jnp.float32)],
        compiler_params=pltpu.CompilerParams(
            vmem_limit_bytes=VMEM_LIMIT, dimension_semantics=("arbitrary",)
        ),
        cost_estimate=pl.CostEstimate(
            flops=4 * freq_count * rows * samples,
            bytes_accessed=2 * rows * samples,
            transcendentals=0,
        ),
    )(traces2, table)


def adapt_kernel(
    freq_count, shots, points,
    near_ref, operator_ref, edge_ref, spectra_ref, basis_ref, traces_ref, out_ref,
    predicted, lines, split_basis,
):
    step = pl.program_id(0)
    local = operator_ref.shape[2]
    lanes = 2 * shots
    terms = 2 * freq_count

    def combined(real_rows, imag_rows):
        sign = jnp.where(
            lax.broadcasted_iota(jnp.int32, real_rows.shape, 1) < shots, -1.0, 1.0
        )
        return real_rows + sign * swap_halves(imag_rows, shots)

    @pl.when(step == 0)
    def _():
        basis = basis_ref[...]
        high = basis.astype(jnp.bfloat16)
        split_basis[0:terms, :] = high
        split_basis[terms : 2 * terms, :] = high
        split_basis[2 * terms :, :] = (basis - high.astype(jnp.float32)).astype(jnp.bfloat16)

    @pl.when(step < freq_count)
    def _():
        spectra = spectra_ref[:, 0].reshape(-1, lanes)
        real = jnp.dot(operator_ref[0, 0], spectra, preferred_element_type=jnp.float32)
        imag = jnp.dot(operator_ref[0, 1], spectra, preferred_element_type=jnp.float32)
        predicted[step, 8 : 8 + local, :] = combined(real, imag)
        edge = jnp.dot(edge_ref[0], spectra, preferred_element_type=jnp.float32)
        predicted[step, 0:8, :] = combined(edge[0:8], edge[8:16])

    @pl.when(step == freq_count - 1)
    def _():
        for f in range(freq_count):
            mine = predicted[f, 8 : 8 + local, :]
            lines[pl.ds(HALO * freq_count + f, local, stride=freq_count), :] = mine
            for h in range(HALO):
                before = h * freq_count + f
                lines[before : before + 1, :] = predicted[f, h : h + 1, :]
                after = (HALO + local + h) * freq_count + f
                lines[after : after + 1, :] = predicted[f, HALO + h : HALO + h + 1, :]

    @pl.when(step >= freq_count)
    def _():
        start = (step - freq_count) * points
        low = lax.broadcasted_iota(jnp.int32, (freq_count, lanes), 1) < shots

        def mixed(point):
            own = pl.multiple_of((point + HALO) * freq_count, freq_count)
            other = pl.multiple_of((point + HALO + near_ref[point]) * freq_count, freq_count)
            return lines[pl.ds(own, freq_count), :] + 0.5 * lines[pl.ds(other, freq_count), :]

        group = 8
        for part in range(points // group):
            reals, imags = [], []
            for pair in range(group // 2):
                first = mixed(start + part * group + 2 * pair)
                second = mixed(start + part * group + 2 * pair + 1)
                reals.append(jnp.where(low, first, swap_halves(second, shots)))
                imags.append(jnp.where(low, swap_halves(first, shots), second))
            terms_by_row = jnp.concatenate(
                [jnp.concatenate(reals, axis=1), jnp.concatenate(imags, axis=1)], axis=0
            )
            high = terms_by_row.astype(jnp.bfloat16)
            rest = (terms_by_row - high.astype(jnp.float32)).astype(jnp.bfloat16)
            left = jnp.concatenate([high, rest, high], axis=0)
            adapted = lax.dot_general(
                left, split_basis[...], TN_DIMS, preferred_element_type=jnp.float32
            )
            rows = slice(part * group * shots, (part + 1) * group * shots)
            out_ref[rows, :] = (traces_ref[rows, :].astype(jnp.float32) - adapted).astype(
                out_ref.dtype
            )


def adapt(near, operator, edge, spectra, basis, traces2, shots, points):
    freq_count, _, local, sources = operator.shape
    rows, samples = traces2.shape
    parts = spectra.shape[0]
    block = points * shots

    def f_of(i):
        return jnp.minimum(i, freq_count - 1)

    def row_of(i):
        return jnp.maximum(i - freq_count, 0)

    return pl.pallas_call(
        functools.partial(adapt_kernel, freq_count, shots, points),
        out_shape=jax.ShapeDtypeStruct((rows, samples), jnp.bfloat16),
        grid=(freq_count + local // points,),
        in_specs=[
            pl.BlockSpec(memory_space=pltpu.SMEM),
            pl.BlockSpec((1, 2, local, sources), lambda i: (f_of(i), 0, 0, 0)),
            pl.BlockSpec((1, 16, sources), lambda i: (f_of(i), 0, 0)),
            pl.BlockSpec((parts, 1, local, 2 * shots), lambda i: (0, f_of(i), 0, 0)),
            pl.BlockSpec((2 * freq_count, samples), lambda i: (0, 0)),
            pl.BlockSpec((block, samples), lambda i: (row_of(i), 0)),
        ],
        out_specs=pl.BlockSpec((block, samples), lambda i: (row_of(i), 0)),
        scratch_shapes=[
            pltpu.VMEM((freq_count, local + 8, 2 * shots), jnp.float32),
            pltpu.VMEM(((local + 2 * HALO) * freq_count, 2 * shots), jnp.float32),
            pltpu.VMEM((6 * freq_count, samples), jnp.bfloat16),
        ],
        compiler_params=pltpu.CompilerParams(
            vmem_limit_bytes=VMEM_LIMIT, dimension_semantics=("arbitrary",)
        ),
    )(near, operator, edge, spectra, basis, traces2)


def on_device(traces, operator, freq_bins, win_lengths, coefficients, neighbour):
    local, shots, samples = traces.shape
    freq_count = freq_bins.shape[0]
    size = lax.axis_size("surf")
    points = 16
    up = [(i, i + 1) for i in range(size - 1)]
    down = [(j, i) for i, j in up]
    before = lax.ppermute(operator[local - HALO :], "surf", up)
    after = lax.ppermute(operator[:HALO], "surf", down)
    edge = jnp.concatenate([before, after], axis=0).transpose(1, 2, 0, 3)
    edge = jnp.pad(edge, ((0, 0), (0, 0), (0, 8 - 2 * HALO), (0, 0)))
    edge = edge.reshape(freq_count, 16, operator.shape[3])

    angles = angle_grid(freq_bins, samples)
    table = jnp.concatenate([jnp.cos(angles.T), -jnp.sin(angles.T)], axis=0)
    norm = (2.0 * freq_count * samples) ** (-0.5)
    basis = matching(norm * table, coefficients, win_lengths)

    traces2 = traces.reshape(local * shots, samples)
    spectra = forward(traces2, table.astype(jnp.bfloat16), freq_count, shots, points)
    gathered = lax.all_gather(spectra, "surf")
    by_freq = operator.transpose(1, 2, 0, 3)
    out = adapt(neighbour, by_freq, edge, gathered, basis, traces2, shots, points)
    return out.reshape(local, shots, samples)


def solution(mesh):
    return jax.shard_map(
        on_device,
        mesh=mesh,
        in_specs=(P("surf", "group", None), P("surf", None, None, None), P(), P(), P(), P("surf")),
        out_specs=P("surf", "group", None),
        check_vma=False,
    )
```

time: 431 us -> 161 us (0.37)
  matrix products: 155 us -> 0.25 us
  waiting for transfers between devices: 182 us -> 38.7 us
  Pallas kernels: 0 us -> 67.4 us
  other arithmetic: 34.4 us -> 3.7 us
  local copies, waits for them, and re-layouts: 39.2 us -> 32.9 us
    reduce_scatter x1 -> x0, waiting for transfers between devices: 178 us -> none  [on_device(): lax.psum_scatter(combine_complex_parts(products).reshape(lax.axis_size('s...]
    dot_general x4 -> x1, matrix products: 155 us -> 0.25 us  [matching(): jnp.dot(coefficients.T, membership, precision=lax.Precision.HIGHEST)]
    pallas_call x0 -> x2, Pallas kernels: none -> 67.4 us  [the longest x1 46.2 us: adapt(): pl.pallas_call(functools.partial(adapt_kernel, freq_count, shots, points)...]
    all_gather x0 -> x1, waiting for transfers between devices: none -> 38.7 us  [on_device(): gathered = lax.all_gather(spectra, 'surf')]
    convert_element_type x2 -> x0, local copies, waits for them, and re-layouts: 30.8 us -> none  [the longest x1 30.8 us: on_device(): return (traces.astype(jnp.float32) - adapted).astype(jnp.bfloat16)]
    unnamed x8 -> x6, local copies, waits for them, and re-layouts: 0.64 us -> 30.1 us
    add x2 -> x1, other arithmetic: 13.5 us -> 1.2 us  [matching(): summed + per_sample[lag_index][None] * padded[:, lag_index:lag_index + sa...]
    sub x1 -> x0, other arithmetic: 11.1 us -> none  [combine_complex_parts(): real_part = products[:, :, 0, 0] - products[:, :, 1, 1]]
  transfers between devices with their start and end apart: 3 -> 3, of which waited for: 2 -> 1; matrix products, arithmetic and copies ran while one was open for 0% -> 22% of each run, Pallas kernels for 0% -> 0%
where the time goes in v1:
time: 161 us; the launch traced here: 160 us
  Pallas kernels  67.4 us (42%)
  waiting for transfers between devices  38.7 us (24%)
  local copies, waits for them, and re-layouts  32.9 us (20%)
  between operations  13.5 us (8%)
  starting transfers between devices  3.71 us (2%)
  other arithmetic  3.7 us (2%)
    pallas_call x1, Pallas kernels, adapt(): pl.pallas_call(functools.partial(adapt_kernel, freq_count, shots, points)...  46.2 us
    all_gather x1, waiting for transfers between devices, on_device(): gathered = lax.all_gather(spectra, 'surf')  38.7 us
    unnamed x6, local copies, waits for them, and re-layouts  30.1 us
    pallas_call x1, Pallas kernels, forward(): pl.pallas_call(functools.partial(forward_kernel, freq_count, shots), out_...  21.2 us
  transfers between devices with their start and end apart: 3, of which 1 were waited for; matrix products, arithmetic and copies ran while one was open for 22% of the time, Pallas kernels for 0%

profile of v1, /device:TPU:0, one launch (start us, length us, event | category | flops | bytes accessed | tf_op | source)
XLA Modules:
  0.0 160.2 jit_solution(10284409601961354815)
XLA Ops:
  6.5 0.0 copy-start
  6.5 0.0 copy-start.1
  6.5 0.0 all-gather.3.cloned.1.call-start
  6.5 0.9 fusion.69
  7.4 0.6 fusion.61.table_ref
  8.1 21.2 %shard_map.64 = bf16[8,256,128]{2,1,0:T(8,128)(2,1)} custom-call(bf16[16384,1024]{1,0:T(8,128)(2,1)} %bitcast.45, bf16[16,1024]{1,0:T(8,128)(2,1)} %fusion.61.table_ref), custom_call_target="tpu_custom_call" | custom-call | flops 536870912 | bytes 33554432 | tf_op jit(solution)/shard_map/pallas_call | solution.py:67
  29.2 0.0 all-gather.3.cloned.1.call-update
  29.3 1.5 fusion.70
  30.7 2.4 %collective-permute-start = (bf16[2,8,2,4096]{3,2,1,0:T(2,128)(2,1)S(1)}, bf16[2,8,2,4096]{3,2,1,0:T(2,128)(2,1)S(1)}, u32[]{:S(2)}, u32[]{:S(2)}) collective-permute-start(bf16[2,8,2,4096]{3,2,1,0:T(2,128)(2,1)S(1)} %get-tuple-element.5), channel_id=1, source_target_pairs={{0,1},{1,2},{2,3},{3,4},{4,5},{5,6},{6,7},{7,8},{8,9},{9,10},{10,1... | collective-permute-start | bytes 786440 | tf_op jit(solution)/shard_map/ppermute | solution.py:208
  33.1 1.3 collective-permute-start.1
  34.4 0.0 copy-done.1
  34.4 0.1 copy.18
  34.6 0.1 reduce
  34.7 0.1 convert_reduce_fusion
  34.8 0.0 copy-done
  34.8 0.3 convolution_bitcast_fusion
  35.1 0.1 fusion.71
  35.2 29.7 %copy.21 = bf16[256,8,2,4096]{3,0,2,1:T(8,128)(2,1)} copy(bf16[256,8,2,4096]{3,2,1,0:T(2,128)(2,1)} %param.7) | data formatting | bytes 67108864 | tf_op args[1]
  64.9 1.2 fusion.53.basis_ref
  66.1 0.0 collective-permute-done
  66.1 0.0 collective-permute-done.1
  66.1 0.7 maximum_bitcast_fusion
  66.8 0.4 copy.19
  67.2 1.2 pad_bitcast_fusion.edge_ref
  68.4 38.7 %all-gather.3.cloned.1.call-done = bf16[128,256,128]{2,1,0:T(8,128)(2,1)} async-done(((bf16[8,256,128]{2,1,0:T(8,128)(2,1)}), bf16[128,256,128]{2,1,0:T(8,128)(2,1)}) %all-gather.3.cloned.1.call-update) | async-done | bytes 8388624 | tf_op jit(solution)/shard_map/all_gather | solution.py:221
  107.1 46.2 %shard_map.65 = bf16[16384,1024]{1,0:T(8,128)(2,1)} custom-call(s32[256]{0:T(256)} %near_ref.1, bf16[8,2,256,4096]{3,2,1,0:T(8,128)(2,1)} %bitcast.47, bf16[8,16,4096]{2,1,0:T(8,128)(2,1)} %pad_bitcast_fusion.edge_ref, bf16[16,8,256,128]{3,2,1,0:T(8,128)(2,1)} %bitcast.48, f32[16,1024]{1,0:T(8,128)} %fusion.53.basis_ref, bf16[16384,1024]{1,0:T(8,128)(2,1)} %bitcast.46), custom_call_target="tpu_custom_call" | custom-call | tf_op jit(solution)/shard_map/pallas_call | solution.py:177
  (3 shorter events, 0.1 us)
Async XLA Ops:
  6.5 28.2 %copy-start = (f32[16,31]{1,0:T(8,128)S(1)}, f32[16,31]{1,0:T(8,128)}, u32[]{:S(2)}) copy-start(f32[16,31]{1,0:T(8,128)} %param.10) | copy-start | bytes 5956
  6.5 27.9 %copy-start.1 = (s32[16]{0:T(128)S(1)}, s32[16]{0:T(128)}, u32[]{:S(2)}) copy-start(s32[16]{0:T(128)} %param.9) | copy-start | bytes 196
  6.5 100.6 %all-gather.3.cloned.1.call-start = ((), (), s32[]{:S(2)}) async-start(), calls=%async_computation | async-start | bytes 8912896 | tf_op jit(solution)/shard_map/all_gather | solution.py:221
  30.7 35.4 %collective-permute-start = (bf16[2,8,2,4096]{3,2,1,0:T(2,128)(2,1)S(1)}, bf16[2,8,2,4096]{3,2,1,0:T(2,128)(2,1)S(1)}, u32[]{:S(2)}, u32[]{:S(2)}) collective-permute-start(bf16[2,8,2,4096]{3,2,1,0:T(2,128)(2,1)S(1)} %get-tuple-element.5), channel_id=1, source_target_pairs={{0,1},{1,2},{2,3},{3,4},{4,5},{5,6},{6,7},{7,8},{8,9},{9,10},{10,1... | collective-permute-start | bytes 786440 | tf_op jit(solution)/shard_map/ppermute | solution.py:208
  33.1 33.0 %collective-permute-start.1 = (bf16[2,8,2,4096]{3,2,1,0:T(2,128)(2,1)S(1)}, bf16[2,8,2,4096]{3,2,1,0:T(2,128)(2,1)S(1)}, u32[]{:S(2)}, u32[]{:S(2)}) collective-permute-start(bf16[2,8,2,4096]{3,2,1,0:T(2,128)(2,1)S(1)} %get-tuple-element.6), channel_id=1, source_target_pairs={{1,0},{2,1},{3,2},{4,3},{5,4},{6,5},{7,6},{8,7},{9,8},{10,9},{11,1... | collective-permute-start | bytes 786440 | tf_op jit(solution)/shard_map/ppermute | solution.py:209
Sparse Core Ops, SparseCore 0:
  29.4 77.6 all-gather.2

commit v2 on v1

--- a/solution.py
+++ b/solution.py
@@ -61,15 +61,17 @@
         out_ref[f] = lines[pl.ds(f, points, stride=freq_count), :].astype(out_ref.dtype)
 
 
-def forward(traces2, table, freq_count, shots, points):
+def forward(traces2, table, freq_count, shots, points, chunk, chunks):
     rows, samples = traces2.shape
+    rows = rows // chunks
     local = rows // shots
+    first = chunk * (local // points)
     return pl.pallas_call(
         functools.partial(forward_kernel, freq_count, shots),
         out_shape=jax.ShapeDtypeStruct((freq_count, local, 2 * shots), jnp.bfloat16),
         grid=(local // points,),
         in_specs=[
-            pl.BlockSpec((points * shots, samples), lambda i: (i, 0)),
+            pl.BlockSpec((points * shots, samples), lambda i: (first + i, 0)),
             pl.BlockSpec((2 * freq_count, samples), lambda i: (0, 0)),
         ],
         out_specs=pl.BlockSpec((freq_count, points, 2 * shots), lambda i: (0, i, 0)),
@@ -85,21 +87,84 @@
     )(traces2, table)
 
 
-def adapt_kernel(
-    freq_count, shots, points,
-    near_ref, operator_ref, edge_ref, spectra_ref, basis_ref, traces_ref, out_ref,
-    predicted, lines, split_basis,
-):
+def combined(real_rows, imag_rows, shots):
+    low = lax.broadcasted_iota(jnp.int32, real_rows.shape, 1) < shots
+    return real_rows + jnp.where(low, -1.0, 1.0) * swap_halves(imag_rows, shots)
+
+
+def products(operator_refs, edge_refs, spectra_ref, shots):
+    spectra = spectra_ref[:, 0].reshape(-1, 2 * shots)
+    planes = [
+        jnp.concatenate([ref[0, part] for ref in operator_refs], axis=1) for part in range(2)
+    ]
+    planes.append(jnp.concatenate([ref[0] for ref in edge_refs], axis=1))
+    real, imag, edge = [
+        jnp.dot(plane, spectra, preferred_element_type=jnp.float32) for plane in planes
+    ]
+    return combined(real, imag, shots), combined(edge[0:8], edge[8:16], shots)
+
+
+def partial_kernel(shots, pieces, *refs):
+    operator_refs, edge_refs = refs[:pieces], refs[pieces : 2 * pieces]
+    spectra_ref, out_ref = refs[2 * pieces :]
+    local = operator_refs[0].shape[2]
+    main, edge = products(operator_refs, edge_refs, spectra_ref, shots)
+    out_ref[0, 8 : 8 + local, :] = main
+    out_ref[0, 0:8, :] = edge
+
+
+def source_specs(local, sources, parts, chunk, chunks, f_of):
+    pieces = parts if chunks > 1 else 1
+    width = sources // (pieces * chunks)
+
+    def column(piece):
+        return piece * chunks + chunk
+
+    operator_specs = [
+        pl.BlockSpec((1, 2, local, width), lambda i, c=column(p): (f_of(i), 0, 0, c))
+        for p in range(pieces)
+    ]
+    edge_specs = [
+        pl.BlockSpec((1, 16, width), lambda i, c=column(p): (f_of(i), 0, c))
+        for p in range(pieces)
+    ]
+    return pieces, operator_specs, edge_specs
+
+
+def partial_product(operator, edge, spectra, shots, chunk, chunks):
+    freq_count, _, local, sources = operator.shape
+    parts, _, mine, lanes = spectra.shape
+    pieces, operator_specs, edge_specs = source_specs(
+        local, sources, parts, chunk, chunks, lambda i: i
+    )
+    return pl.pallas_call(
+        functools.partial(partial_kernel, shots, pieces),
+        out_shape=jax.ShapeDtypeStruct((freq_count, local + 8, lanes), jnp.float32),
+        grid=(freq_count,),
+        in_specs=operator_specs
+        + edge_specs
+        + [pl.BlockSpec((parts, 1, mine, lanes), lambda i: (0, i, 0, 0))],
+        out_specs=pl.BlockSpec((1, local + 8, lanes), lambda i: (i, 0, 0)),
+        compiler_params=pltpu.CompilerParams(
+            vmem_limit_bytes=VMEM_LIMIT, dimension_semantics=("arbitrary",)
+        ),
+        cost_estimate=pl.CostEstimate(
+            flops=4 * freq_count * local * (sources // chunks) * lanes,
+            bytes_accessed=4 * freq_count * local * (sources // chunks),
+            transcendentals=0,
+        ),
+    )(*([operator] * pieces), *([edge] * pieces), spectra)
+
+
+def adapt_kernel(freq_count, shots, points, pieces, partials, *refs):
+    near_ref, operator_refs, edge_refs = refs[0], refs[1 : 1 + pieces], refs[1 + pieces : 1 + 2 * pieces]
+    spectra_ref = refs[1 + 2 * pieces]
+    partial_refs = refs[2 + 2 * pieces : 2 + 2 * pieces + partials]
+    basis_ref, traces_ref, out_ref, predicted, lines, split_basis = refs[2 + 2 * pieces + partials :]
     step = pl.program_id(0)
-    local = operator_ref.shape[2]
+    local = operator_refs[0].shape[2]
     lanes = 2 * shots
     terms = 2 * freq_count
-
-    def combined(real_rows, imag_rows):
-        sign = jnp.where(
-            lax.broadcasted_iota(jnp.int32, real_rows.shape, 1) < shots, -1.0, 1.0
-        )
-        return real_rows + sign * swap_halves(imag_rows, shots)
 
     @pl.when(step == 0)
     def _():
@@ -111,12 +176,12 @@
 
     @pl.when(step < freq_count)
     def _():
-        spectra = spectra_ref[:, 0].reshape(-1, lanes)
-        real = jnp.dot(operator_ref[0, 0], spectra, preferred_element_type=jnp.float32)
-        imag = jnp.dot(operator_ref[0, 1], spectra, preferred_element_type=jnp.float32)
-        predicted[step, 8 : 8 + local, :] = combined(real, imag)
-        edge = jnp.dot(edge_ref[0], spectra, preferred_element_type=jnp.float32)
-        predicted[step, 0:8, :] = combined(edge[0:8], edge[8:16])
+        main, edge = products(operator_refs, edge_refs, spectra_ref, shots)
+        for ref in partial_refs:
+            main = main + ref[0, 8 : 8 + local, :]
+            edge = edge + ref[0, 0:8, :]
+        predicted[step, 8 : 8 + local, :] = main
+        predicted[step, 0:8, :] = edge
 
     @pl.when(step == freq_count - 1)
     def _():
@@ -162,10 +227,10 @@
             )
 
 
-def adapt(near, operator, edge, spectra, basis, traces2, shots, points):
+def adapt(near, operator, edge, spectra, partial, basis, traces2, shots, points, chunk, chunks):
     freq_count, _, local, sources = operator.shape
     rows, samples = traces2.shape
-    parts = spectra.shape[0]
+    parts, _, mine, lanes = spectra.shape
     block = points * shots
 
     def f_of(i):
@@ -174,35 +239,40 @@
     def row_of(i):
         return jnp.maximum(i - freq_count, 0)
 
+    pieces, operator_specs, edge_specs = source_specs(local, sources, parts, chunk, chunks, f_of)
+    partial_specs = [
+        pl.BlockSpec((1, local + 8, lanes), lambda i: (f_of(i), 0, 0)) for _ in partial
+    ]
     return pl.pallas_call(
-        functools.partial(adapt_kernel, freq_count, shots, points),
+        functools.partial(adapt_kernel, freq_count, shots, points, pieces, len(partial)),
         out_shape=jax.ShapeDtypeStruct((rows, samples), jnp.bfloat16),
         grid=(freq_count + local // points,),
-        in_specs=[
-            pl.BlockSpec(memory_space=pltpu.SMEM),
-            pl.BlockSpec((1, 2, local, sources), lambda i: (f_of(i), 0, 0, 0)),
-            pl.BlockSpec((1, 16, sources), lambda i: (f_of(i), 0, 0)),
-            pl.BlockSpec((parts, 1, local, 2 * shots), lambda i: (0, f_of(i), 0, 0)),
+        in_specs=[pl.BlockSpec(memory_space=pltpu.SMEM)]
+        + operator_specs
+        + edge_specs
+        + [pl.BlockSpec((parts, 1, mine, lanes), lambda i: (0, f_of(i), 0, 0))]
+        + partial_specs
+        + [
             pl.BlockSpec((2 * freq_count, samples), lambda i: (0, 0)),
             pl.BlockSpec((block, samples), lambda i: (row_of(i), 0)),
         ],
         out_specs=pl.BlockSpec((block, samples), lambda i: (row_of(i), 0)),
         scratch_shapes=[
-            pltpu.VMEM((freq_count, local + 8, 2 * shots), jnp.float32),
-            pltpu.VMEM(((local + 2 * HALO) * freq_count, 2 * shots), jnp.float32),
+            pltpu.VMEM((freq_count, local + 8, lanes), jnp.float32),
+            pltpu.VMEM(((local + 2 * HALO) * freq_count, lanes), jnp.float32),
             pltpu.VMEM((6 * freq_count, samples), jnp.bfloat16),
         ],
         compiler_params=pltpu.CompilerParams(
             vmem_limit_bytes=VMEM_LIMIT, dimension_semantics=("arbitrary",)
         ),
-    )(near, operator, edge, spectra, basis, traces2)
+    )(near, *([operator] * pieces), *([edge] * pieces), spectra, *partial, basis, traces2)
 
 
 def on_device(traces, operator, freq_bins, win_lengths, coefficients, neighbour):
     local, shots, samples = traces.shape
     freq_count = freq_bins.shape[0]
     size = lax.axis_size("surf")
-    points = 16
+    points = 32
     up = [(i, i + 1) for i in range(size - 1)]
     down = [(j, i) for i, j in up]
     before = lax.ppermute(operator[local - HALO :], "surf", up)
@@ -217,10 +287,20 @@
     basis = matching(norm * table, coefficients, win_lengths)
 
     traces2 = traces.reshape(local * shots, samples)
-    spectra = forward(traces2, table.astype(jnp.bfloat16), freq_count, shots, points)
-    gathered = lax.all_gather(spectra, "surf")
+    bf16_table = table.astype(jnp.bfloat16)
+    chunks = 2 if local % 256 == 0 else 1
+    gathered = []
+    for chunk in range(chunks):
+        spectra = forward(traces2, bf16_table, freq_count, shots, points, chunk, chunks)
+        gathered.append(lax.all_gather(spectra, "surf"))
     by_freq = operator.transpose(1, 2, 0, 3)
-    out = adapt(neighbour, by_freq, edge, gathered, basis, traces2, shots, points)
+    partial = []
+    for chunk in range(chunks - 1):
+        partial.append(partial_product(by_freq, edge, gathered[chunk], shots, chunk, chunks))
+    out = adapt(
+        neighbour, by_freq, edge, gathered[-1], partial, basis, traces2,
+        shots, points, chunks - 1, chunks,
+    )
     return out.reshape(local, shots, samples)
 
 

time: 161 us -> 169 us (1.050)
  waiting for transfers between devices: 38.7 us -> 44.2 us
  Pallas kernels: 67.4 us -> 70 us
    all_gather x1 -> x2, waiting for transfers between devices: 38.7 us -> 44.2 us  [on_device(): gathered.append(lax.all_gather(spectra, 'surf'))]
    pallas_call x1 -> x2, Pallas kernels: 46.2 us -> 51.6 us  [the longest x1 38.7 us: adapt(): pl.pallas_call(functools.partial(adapt_kernel, freq_count, shots, points,...]
    pallas_call x1 -> x2, Pallas kernels: 21.2 us -> 18.4 us  [forward(): pl.pallas_call(functools.partial(forward_kernel, freq_count, shots), out_...]
    unnamed x6 -> x8, local copies, waits for them, and re-layouts: 30.1 us -> 30.1 us
  transfers between devices with their start and end apart: 3 -> 4, of which waited for: 1 -> 2; matrix products, arithmetic and copies ran while one was open for 22% -> 21% of each run, Pallas kernels for 0% -> 13%
where the time goes in v2:
time: 169 us; the launch traced here: 168 us
  Pallas kernels  70 us (41%)
  waiting for transfers between devices  44.2 us (26%)
  local copies, waits for them, and re-layouts  33 us (20%)
  between operations  13.5 us (8%)
  starting transfers between devices  3.75 us (2%)
  other arithmetic  3.69 us (2%)
    all_gather x2, waiting for transfers between devices, on_device(): gathered.append(lax.all_gather(spectra, 'surf'))  44.2 us
    pallas_call x1, Pallas kernels, adapt(): pl.pallas_call(functools.partial(adapt_kernel, freq_count, shots, points,...  38.7 us
    unnamed x8, local copies, waits for them, and re-layouts  30.1 us
    pallas_call x2, Pallas kernels, forward(): pl.pallas_call(functools.partial(forward_kernel, freq_count, shots), out_...  18.4 us
    pallas_call x1, Pallas kernels, partial_product(): pl.pallas_call(functools.partial(partial_kernel, shots, pieces), out_shap...  12.9 us
  transfers between devices with their start and end apart: 4, of which 2 were waited for; matrix products, arithmetic and copies ran while one was open for 21% of the time, Pallas kernels for 13%

profile of v2, /device:TPU:0, one launch (start us, length us, event | category | flops | bytes accessed | tf_op | source)
XLA Modules:
  0.0 168.3 jit_solution(6799274745038409412)
XLA Ops:
  6.5 0.0 copy-start
  6.5 0.0 all-gather.7.cloned.1.call-start
  6.5 0.9 fusion.69
  7.4 0.6 fusion.61.table_ref
  8.0 0.0 copy-start.2
  8.0 9.2 %shard_map.65 = bf16[8,128,128]{2,1,0:T(8,128)(2,1)} custom-call(bf16[16384,1024]{1,0:T(8,128)(2,1)} %bitcast.78, bf16[16,1024]{1,0:T(8,128)(2,1)} %fusion.61.table_ref), custom_call_target="tpu_custom_call" | custom-call | flops 268435456 | bytes 16777216 | tf_op jit(solution)/shard_map/pallas_call | solution.py:69
  17.2 0.0 all-gather.7.cloned.1.call-update
  17.3 0.0 all-gather.5.cloned.1.call-start
  17.3 9.2 %shard_map.64 = bf16[8,128,128]{2,1,0:T(8,128)(2,1)} custom-call(bf16[16384,1024]{1,0:T(8,128)(2,1)} %bitcast.79, bf16[16,1024]{1,0:T(8,128)(2,1)} %fusion.61.table_ref), custom_call_target="tpu_custom_call" | custom-call | flops 268435456 | bytes 16777216 | tf_op jit(solution)/shard_map/pallas_call | solution.py:69
  26.5 0.0 all-gather.5.cloned.1.call-update
  26.5 1.5 fusion.70
  28.0 2.4 %collective-permute-start = (bf16[2,8,2,4096]{3,2,1,0:T(2,128)(2,1)S(1)}, bf16[2,8,2,4096]{3,2,1,0:T(2,128)(2,1)S(1)}, u32[]{:S(2)}, u32[]{:S(2)}) collective-permute-start(bf16[2,8,2,4096]{3,2,1,0:T(2,128)(2,1)S(1)} %get-tuple-element.5), channel_id=1, source_target_pairs={{0,1},{1,2},{2,3},{3,4},{4,5},{5,6},{6,7},{7,8},{8,9},{9,10},{10,1... | collective-permute-start | bytes 786440 | tf_op jit(solution)/shard_map/ppermute | solution.py:278
  30.4 1.3 collective-permute-start.1
  31.7 0.0 copy-done.2
  31.7 0.1 copy.18
  31.8 0.1 reduce
  32.0 0.1 convert_reduce_fusion
  32.0 0.0 copy-done
  32.1 0.3 convolution_bitcast_fusion
  32.4 0.1 fusion.71
  32.4 29.7 %copy.21 = bf16[256,8,2,4096]{3,0,2,1:T(8,128)(2,1)} copy(bf16[256,8,2,4096]{3,2,1,0:T(2,128)(2,1)} %param.7) | data formatting | bytes 67108864 | tf_op args[1]
  62.2 1.2 fusion.53.refs_35_
  63.4 0.0 collective-permute-done
  63.4 0.0 collective-permute-done.1
  63.4 0.7 maximum_bitcast_fusion
  64.0 0.4 copy.19
  64.5 1.2 pad_bitcast_fusion.refs_16_.refs_17_.refs_18_.refs_19_.refs_20_.refs_21_.refs_22_.refs_23_.refs_24_.refs_25_.refs_26_.refs_27_.refs_28_.refs_29_.refs_30_.refs_31_.refs_32_
  65.7 5.9 %all-gather.7.cloned.1.call-done = bf16[128,128,128]{2,1,0:T(8,128)(2,1)} async-done(((bf16[8,128,128]{2,1,0:T(8,128)(2,1)}), bf16[128,128,128]{2,1,0:T(8,128)(2,1)}) %all-gather.7.cloned.1.call-update) | async-done | bytes 4194320 | tf_op jit(solution)/shard_map/all_gather | solution.py:295
  71.6 12.9 %shard_map.66.refs_34_ = f32[8,264,128]{2,1,0:T(8,128)} custom-call(bf16[8,2,256,4096]{3,2,1,0:T(8,128)(2,1)} %bitcast.61, bf16[8,2,256,4096]{3,2,1,0:T(8,128)(2,1)} %bitcast.47, bf16[8,2,256,4096]{3,2,1,0:T(8,128)(2,1)} %bitcast.48, bf16[8,2,256,4096]{3,2,1,0:T(8,128)(2,1)} %bitcast.49, bf16[8,2,256,4096]{3,2,1,0:T(8,128)(2,1)} %bitcast.50, ...), custom_call_target="tpu_custom_call" | custom-call | flops 2147483648 | bytes 16777216 | tf_op jit(solution)/shard_map/pallas_call | solution.py:140
  84.5 38.2 %all-gather.5.cloned.1.call-done = bf16[128,128,128]{2,1,0:T(8,128)(2,1)} async-done(((bf16[8,128,128]{2,1,0:T(8,128)(2,1)}), bf16[128,128,128]{2,1,0:T(8,128)(2,1)}) %all-gather.5.cloned.1.call-update) | async-done | bytes 4194320 | tf_op jit(solution)/shard_map/all_gather | solution.py:295
  122.8 0.0 copy-start.1
  122.8 38.7 %shard_map.67 = bf16[16384,1024]{1,0:T(8,128)(2,1)} custom-call(s32[256]{0:T(256)} %refs_0_.1, bf16[8,2,256,4096]{3,2,1,0:T(8,128)(2,1)} %bitcast.62, bf16[8,2,256,4096]{3,2,1,0:T(8,128)(2,1)} %bitcast.63, bf16[8,2,256,4096]{3,2,1,0:T(8,128)(2,1)} %bitcast.64, bf16[8,2,256,4096]{3,2,1,0:T(8,128)(2,1)} %bitcast.65, bf16[8,2,256,4096]{3,2,1,0:T(8,128)(2,1)} %bitcast.66, ...), custom_call_target="tpu_custom_call" | custom-call | tf_op jit(solution)/shard_map/pallas_call | solution.py:246
  161.5 0.0 copy-done.1
  (3 shorter events, 0.1 us)
Async XLA Ops:
  6.5 25.5 %copy-start = (f32[16,31]{1,0:T(8,128)S(1)}, f32[16,31]{1,0:T(8,128)}, u32[]{:S(2)}) copy-start(f32[16,31]{1,0:T(8,128)} %param.10) | copy-start | bytes 5956
  6.5 65.1 %all-gather.7.cloned.1.call-start = ((), (), s32[]{:S(2)}) async-start(), calls=%async_computation.1 | async-start | bytes 4456448 | tf_op jit(solution)/shard_map/all_gather | solution.py:295
  8.0 23.7 %copy-start.2 = (s32[16]{0:T(128)S(1)}, s32[16]{0:T(128)}, u32[]{:S(2)}) copy-start(s32[16]{0:T(128)} %param.9) | copy-start | bytes 196
  17.3 105.5 %all-gather.5.cloned.1.call-start = ((), (), s32[]{:S(2)}) async-start(), calls=%async_computation | async-start | bytes 4456448 | tf_op jit(solution)/shard_map/all_gather | solution.py:295
  28.0 35.4 %collective-permute-start = (bf16[2,8,2,4096]{3,2,1,0:T(2,128)(2,1)S(1)}, bf16[2,8,2,4096]{3,2,1,0:T(2,128)(2,1)S(1)}, u32[]{:S(2)}, u32[]{:S(2)}) collective-permute-start(bf16[2,8,2,4096]{3,2,1,0:T(2,128)(2,1)S(1)} %get-tuple-element.5), channel_id=1, source_target_pairs={{0,1},{1,2},{2,3},{3,4},{4,5},{5,6},{6,7},{7,8},{8,9},{9,10},{10,1... | collective-permute-start | bytes 786440 | tf_op jit(solution)/shard_map/ppermute | solution.py:278
  30.4 33.0 %collective-permute-start.1 = (bf16[2,8,2,4096]{3,2,1,0:T(2,128)(2,1)S(1)}, bf16[2,8,2,4096]{3,2,1,0:T(2,128)(2,1)S(1)}, u32[]{:S(2)}, u32[]{:S(2)}) collective-permute-start(bf16[2,8,2,4096]{3,2,1,0:T(2,128)(2,1)S(1)} %get-tuple-element.6), channel_id=1, source_target_pairs={{1,0},{2,1},{3,2},{4,3},{5,4},{6,5},{7,6},{8,7},{9,8},{10,9},{11,1... | collective-permute-start | bytes 786440 | tf_op jit(solution)/shard_map/ppermute | solution.py:279
  122.8 38.7 %copy-start.1 = (f32[16,31]{1,0:T(8,128)S(1)}, f32[16,31]{1,0:T(8,128)}, u32[]{:S(2)}) copy-start(f32[16,31]{1,0:T(8,128)} %param.10) | copy-start | bytes 5956
Sparse Core Ops, SparseCore 0:
  17.4 54.2 all-gather.6
  73.8 48.9 all-gather.4

commit v3 on v2

--- a/solution.py
+++ b/solution.py
@@ -288,7 +288,7 @@
 
     traces2 = traces.reshape(local * shots, samples)
     bf16_table = table.astype(jnp.bfloat16)
-    chunks = 2 if local % 256 == 0 else 1
+    chunks = 1
     gathered = []
     for chunk in range(chunks):
         spectra = forward(traces2, bf16_table, freq_count, shots, points, chunk, chunks)

time: 169 us -> 154 us (0.911)
  Pallas kernels: 70 us -> 60.5 us
  waiting for transfers between devices: 44.2 us -> 38.7 us
    pallas_call x1 -> x0, Pallas kernels: 12.9 us -> none  [partial_product(): pl.pallas_call(functools.partial(partial_kernel, shots, pieces), out_shap...]
    all_gather x2 -> x1, waiting for transfers between devices: 44.2 us -> 38.7 us  [on_device(): gathered.append(lax.all_gather(spectra, 'surf'))]
    pallas_call x1, Pallas kernels: 38.7 us -> 44 us  [adapt(): pl.pallas_call(functools.partial(adapt_kernel, freq_count, shots, points,...]
    pallas_call x2 -> x1, Pallas kernels: 18.4 us -> 16.5 us  [forward(): pl.pallas_call(functools.partial(forward_kernel, freq_count, shots), out_...]
    unnamed x8 -> x6, local copies, waits for them, and re-layouts: 30.1 us -> 30.1 us
  transfers between devices with their start and end apart: 4 -> 3, of which waited for: 2 -> 1; matrix products, arithmetic and copies ran while one was open for 21% -> 23% of each run, Pallas kernels for 13% -> 0%
where the time goes in v3:
time: 154 us; the launch traced here: 153 us
  Pallas kernels  60.5 us (39%)
  waiting for transfers between devices  38.7 us (25%)
  local copies, waits for them, and re-layouts  32.9 us (21%)
  between operations  13.5 us (9%)
  starting transfers between devices  3.71 us (2%)
  other arithmetic  3.7 us (2%)
    pallas_call x1, Pallas kernels, adapt(): pl.pallas_call(functools.partial(adapt_kernel, freq_count, shots, points,...  44 us
    all_gather x1, waiting for transfers between devices, on_device(): gathered.append(lax.all_gather(spectra, 'surf'))  38.7 us
    unnamed x6, local copies, waits for them, and re-layouts  30.1 us
    pallas_call x1, Pallas kernels, forward(): pl.pallas_call(functools.partial(forward_kernel, freq_count, shots), out_...  16.5 us
  transfers between devices with their start and end apart: 3, of which 1 were waited for; matrix products, arithmetic and copies ran while one was open for 23% of the time, Pallas kernels for 0%

profile of v3, /device:TPU:0, one launch (start us, length us, event | category | flops | bytes accessed | tf_op | source)
XLA Modules:
  0.0 153.3 jit_solution(9247921953049288448)
XLA Ops:
  6.5 0.0 copy-start
  6.5 0.0 copy-start.1
  6.5 0.0 all-gather.3.cloned.1.call-start
  6.5 0.9 fusion.69
  7.4 0.6 fusion.61.table_ref
  8.1 16.5 %shard_map.64 = bf16[8,256,128]{2,1,0:T(8,128)(2,1)} custom-call(bf16[16384,1024]{1,0:T(8,128)(2,1)} %bitcast.45, bf16[16,1024]{1,0:T(8,128)(2,1)} %fusion.61.table_ref), custom_call_target="tpu_custom_call" | custom-call | flops 536870912 | bytes 33554432 | tf_op jit(solution)/shard_map/pallas_call | solution.py:69
  24.6 0.0 all-gather.3.cloned.1.call-update
  24.6 1.5 fusion.70
  26.0 2.4 %collective-permute-start = (bf16[2,8,2,4096]{3,2,1,0:T(2,128)(2,1)S(1)}, bf16[2,8,2,4096]{3,2,1,0:T(2,128)(2,1)S(1)}, u32[]{:S(2)}, u32[]{:S(2)}) collective-permute-start(bf16[2,8,2,4096]{3,2,1,0:T(2,128)(2,1)S(1)} %get-tuple-element.5), channel_id=1, source_target_pairs={{0,1},{1,2},{2,3},{3,4},{4,5},{5,6},{6,7},{7,8},{8,9},{9,10},{10,1... | collective-permute-start | bytes 786440 | tf_op jit(solution)/shard_map/ppermute | solution.py:278
  28.5 1.3 collective-permute-start.1
  29.8 0.0 copy-done.1
  29.8 0.1 copy.18
  29.9 0.1 reduce
  30.0 0.1 convert_reduce_fusion
  30.1 0.0 copy-done
  30.1 0.3 convolution_bitcast_fusion
  30.4 0.1 fusion.71
  30.5 29.7 %copy.21 = bf16[256,8,2,4096]{3,0,2,1:T(8,128)(2,1)} copy(bf16[256,8,2,4096]{3,2,1,0:T(2,128)(2,1)} %param.7) | data formatting | bytes 67108864 | tf_op args[1]
  60.2 1.2 fusion.53.refs_4_
  61.4 0.0 collective-permute-done
  61.4 0.0 collective-permute-done.1
  61.4 0.7 maximum_bitcast_fusion
  62.1 0.4 copy.19
  62.5 1.2 pad_bitcast_fusion.refs_2_
  63.7 38.7 %all-gather.3.cloned.1.call-done = bf16[128,256,128]{2,1,0:T(8,128)(2,1)} async-done(((bf16[8,256,128]{2,1,0:T(8,128)(2,1)}), bf16[128,256,128]{2,1,0:T(8,128)(2,1)}) %all-gather.3.cloned.1.call-update) | async-done | bytes 8388624 | tf_op jit(solution)/shard_map/all_gather | solution.py:295
  102.5 44.0 %shard_map.65 = bf16[16384,1024]{1,0:T(8,128)(2,1)} custom-call(s32[256]{0:T(256)} %refs_0_.1, bf16[8,2,256,4096]{3,2,1,0:T(8,128)(2,1)} %bitcast.47, bf16[8,16,4096]{2,1,0:T(8,128)(2,1)} %pad_bitcast_fusion.refs_2_, bf16[16,8,256,128]{3,2,1,0:T(8,128)(2,1)} %bitcast.48, f32[16,1024]{1,0:T(8,128)} %fusion.53.refs_4_, bf16[16384,1024]{1,0:T(8,128)(2,1)} %bitcast.46), custom_call_target="tpu_custom_call" | custom-call | tf_op jit(solution)/shard_map/pallas_call | solution.py:246
  (3 shorter events, 0.1 us)
Async XLA Ops:
  6.5 23.6 %copy-start = (f32[16,31]{1,0:T(8,128)S(1)}, f32[16,31]{1,0:T(8,128)}, u32[]{:S(2)}) copy-start(f32[16,31]{1,0:T(8,128)} %param.10) | copy-start | bytes 5956
  6.5 23.2 %copy-start.1 = (s32[16]{0:T(128)S(1)}, s32[16]{0:T(128)}, u32[]{:S(2)}) copy-start(s32[16]{0:T(128)} %param.9) | copy-start | bytes 196
  6.5 95.9 %all-gather.3.cloned.1.call-start = ((), (), s32[]{:S(2)}) async-start(), calls=%async_computation | async-start | bytes 8912896 | tf_op jit(solution)/shard_map/all_gather | solution.py:295
  26.0 35.4 %collective-permute-start = (bf16[2,8,2,4096]{3,2,1,0:T(2,128)(2,1)S(1)}, bf16[2,8,2,4096]{3,2,1,0:T(2,128)(2,1)S(1)}, u32[]{:S(2)}, u32[]{:S(2)}) collective-permute-start(bf16[2,8,2,4096]{3,2,1,0:T(2,128)(2,1)S(1)} %get-tuple-element.5), channel_id=1, source_target_pairs={{0,1},{1,2},{2,3},{3,4},{4,5},{5,6},{6,7},{7,8},{8,9},{9,10},{10,1... | collective-permute-start | bytes 786440 | tf_op jit(solution)/shard_map/ppermute | solution.py:278
  28.5 33.0 %collective-permute-start.1 = (bf16[2,8,2,4096]{3,2,1,0:T(2,128)(2,1)S(1)}, bf16[2,8,2,4096]{3,2,1,0:T(2,128)(2,1)S(1)}, u32[]{:S(2)}, u32[]{:S(2)}) collective-permute-start(bf16[2,8,2,4096]{3,2,1,0:T(2,128)(2,1)S(1)} %get-tuple-element.6), channel_id=1, source_target_pairs={{1,0},{2,1},{3,2},{4,3},{5,4},{6,5},{7,6},{8,7},{9,8},{10,9},{11,1... | collective-permute-start | bytes 786440 | tf_op jit(solution)/shard_map/ppermute | solution.py:279
Sparse Core Ops, SparseCore 0:
  24.7 77.6 all-gather.2
